TPU v7x, 32 devices: a whole 2x2x4 slice. The times are simulated.
32 devices in a mesh: gx: 2 (over x), gy: 4 (over y, core), gz: 4 (over z).
Axes of the slice: x: 2, y: 2, z: 4, core: 2. Of those that a mesh axis runs over, the one named last changes fastest.
Arguments:
- solution_in: float32 [16, 128, 512], P('gx', 'gy', 'gz'), may hold values from -6 to 6
- residual_in: float32 [16, 128, 512], P('gx', 'gy', 'gz'), may hold values from -12 to 12
- direction_in: float32 [16, 128, 512], P('gx', 'gy', 'gz'), may hold values from -6 to 6
- material: int32 [16, 128, 512], P('gx', 'gy', 'gz'), may hold values from 0 to 7
- cond_table: float32 [8], replicated, may hold values from 0.5 to 4
- cap_table: float32 [8], replicated, may hold values from 0.2 to 1
- gas_flux: float32 [128, 512], P('gy', 'gz'), may hold values from -6 to 6
- supply_map: int32 [128, 512], P('gy', 'gz'), may hold values from 0 to 511, as said below
Outputs:
- solution: float32 [16, 128, 512], P('gx', 'gy', 'gz')
- residual: float32 [16, 128, 512], P('gx', 'gy', 'gz')
- direction: float32 [16, 128, 512], P('gx', 'gy', 'gz')
Inputs may be any that keep to these rules, and one draw needn't show every extreme that they name: `supply_map`: the gas faces are laid out so that the faces held by index q of gz, in their slots t * 128 / 4 to (t + 1) * 128 / 4 - 1, supply solid faces held by index t of gz in the same row; every gas face supplies exactly one solid face of its row.
All inputs are finite; a program needn't handle non-finite values.
Results may differ from a plain program's by a relative error of at most 0.0006.
Values sent between devices are 32-bit elements; how exact they have to be, the bound alone decides.
A program may use at most 64 MiB of HBM per device.

v0:
```python
import jax
import jax.numpy as jnp
from jax import lax
from jax.sharding import PartitionSpec as P

STEPS = 4


def extended(block, sides, width):
    for axis, dim in sides:
        count = lax.axis_size(axis)
        forward = [(i, i + 1) for i in range(count - 1)]
        backward = [(target, source) for source, target in forward]
        low = lax.ppermute(
            lax.slice_in_dim(block, block.shape[dim] - width, None, axis=dim), axis, forward
        )
        high = lax.ppermute(lax.slice_in_dim(block, 0, width, axis=dim), axis, backward)
        block = jnp.concatenate([low, block, high], axis=dim)
    return block


def harmonic(lower_side, upper_side):
    return (
        2.0
        * lower_side
        * upper_side
        / (jnp.where(lower_side > 0, lower_side, 1.0) + jnp.where(upper_side > 0, upper_side, 1.0))
    )


def face_terms(cond):
    return (
        harmonic(cond[:-1], cond[1:]),
        harmonic(cond[:, :-1], cond[:, 1:]),
        harmonic(cond[:, :, :-1], cond[:, :, 1:]),
    )


def operate(values, capacity, conductance):
    result = capacity * values
    face_flow = conductance[0] * (values[1:] - values[:-1])
    result = (
        result
        - jnp.pad(face_flow, ((0, 1), (0, 0), (0, 0)))
        + jnp.pad(face_flow, ((1, 0), (0, 0), (0, 0)))
    )
    face_flow = conductance[1] * (values[:, 1:] - values[:, :-1])
    result = (
        result
        - jnp.pad(face_flow, ((0, 0), (0, 1), (0, 0)))
        + jnp.pad(face_flow, ((0, 0), (1, 0), (0, 0)))
    )
    face_flow = conductance[2] * (values[:, :, 1:] - values[:, :, :-1])
    result = (
        result
        - jnp.pad(face_flow, ((0, 0), (0, 0), (0, 1)))
        + jnp.pad(face_flow, ((0, 0), (0, 0), (1, 0)))
    )
    return result


def lookup_code(codes, table):
    summed = jnp.zeros(codes.shape, jnp.float32)
    for material_id in range(table.shape[0]):
        summed = summed + jnp.where(
            codes == jnp.float32(material_id + 1), table[material_id], jnp.float32(0.0)
        )
    return summed


def spectrum(cond_table, cap_table):
    lowest = jnp.min(cap_table)
    highest = jnp.max(cap_table) + 12.0 * jnp.max(cond_table)
    return (0.5 * (highest + lowest), 0.5 * (highest - lowest))


def next_term(applied, terms, center, half_width):
    shifted = (applied - center * terms[-1]) / half_width
    if len(terms) == 1:
        return shifted
    return 2.0 * shifted - terms[-2]


def shift_matrix(center, half_width, steps):
    dimension = 2 * steps + 1
    matrix = jnp.zeros((dimension, dimension), jnp.float32)
    for offset, length in ((0, steps + 1), (steps + 1, steps)):
        for column in range(length - 1):
            matrix = matrix.at[offset + column, offset + column].set(center)
            matrix = matrix.at[offset + column + 1, offset + column].set(
                half_width if column == 0 else 0.5 * half_width
            )
            if column >= 1:
                matrix = matrix.at[offset + column - 1, offset + column].set(0.5 * half_width)
    return matrix


def coefficients(gram, center, half_width, steps):
    dimension = 2 * steps + 1
    matrix = shift_matrix(center, half_width, steps)
    highest_prec = lax.Precision.HIGHEST

    def gram_product(first_vec, second_vec):
        return jnp.dot(
            first_vec, jnp.dot(gram, second_vec, precision=highest_prec), precision=highest_prec
        )

    direct = jnp.zeros((dimension,), jnp.float32).at[0].set(1.0)
    residue = jnp.zeros((dimension,), jnp.float32).at[steps + 1].set(1.0)
    moved = jnp.zeros((dimension,), jnp.float32)
    norm_now = gram_product(residue, residue)
    for sweep in range(steps):
        mapped = jnp.dot(matrix, direct, precision=highest_prec)
        step_length = norm_now / gram_product(direct, mapped)
        moved = moved + step_length * direct
        residue = residue - step_length * mapped
        norm_next = gram_product(residue, residue)
        direct = residue + norm_next / norm_now * direct
        norm_now = norm_next
    return (moved, residue, direct)


def combine(weights, basis):
    summed = weights[0] * basis[0]
    for position in range(1, len(basis)):
        summed = summed + weights[position] * basis[position]
    return summed


def inside(values, depth):
    return values[depth:-depth, depth:-depth, depth:-depth]


def body(
    solution_in, residual_in, direction_in, material, cond_table, cap_table, gas_flux, supply_map
):
    surface_rows, surface_width = gas_flux.shape
    groups = lax.axis_size("gz")
    segment = surface_width // groups
    arrived = lax.all_to_all(
        gas_flux.reshape(surface_rows, groups, segment),
        "gz",
        split_axis=1,
        concat_axis=1,
        tiled=True,
    )
    arrived = arrived.reshape(surface_rows, surface_width)
    slot = (
        supply_map // surface_width * segment
        + supply_map % surface_width
        - lax.axis_index("gz") * segment
    )
    incoming = jnp.take_along_axis(arrived, slot, axis=1)
    is_top = lax.axis_index("gx") == lax.axis_size("gx") - 1
    start = residual_in.at[-1].add(jnp.where(is_top, incoming, jnp.float32(0.0)))
    codes = (material + 1).astype(jnp.float32)
    center, half_width = spectrum(cond_table, cap_table)
    first = extended(jnp.stack([direction_in, start, codes]), (("gx", 1), ("gy", 2), ("gz", 3)), 1)
    conductance = face_terms(lookup_code(first[2], cond_table))
    capacity_ext = lookup_code(first[2], cap_table)
    dir_terms = [direction_in]
    res_terms = [start]
    dir_applied = inside(operate(first[0], capacity_ext, conductance), 1)
    res_applied = inside(operate(first[1], capacity_ext, conductance), 1)
    res_terms.append(next_term(res_applied, res_terms, center, half_width))
    dir_terms.append(next_term(dir_applied, dir_terms, center, half_width))
    for sweep in range(1, STEPS):
        if sweep < STEPS - 1:
            layered = extended(
                jnp.stack([dir_terms[-1], res_terms[-1]]), (("gx", 1), ("gy", 2), ("gz", 3)), 1
            )
            dir_applied = inside(operate(layered[0], capacity_ext, conductance), 1)
            res_applied = inside(operate(layered[1], capacity_ext, conductance), 1)
            res_terms.append(next_term(res_applied, res_terms, center, half_width))
        else:
            layered = extended(dir_terms[-1], (("gx", 0), ("gy", 1), ("gz", 2)), 1)
            dir_applied = inside(operate(layered, capacity_ext, conductance), 1)
        dir_terms.append(next_term(dir_applied, dir_terms, center, half_width))
    basis = dir_terms + res_terms
    stacked = jnp.stack([term.reshape(-1) for term in basis])
    partial_gram = jnp.dot(stacked, stacked.T, precision=lax.Precision.HIGHEST)
    gram = lax.psum(partial_gram, ("gx", "gy", "gz"))
    moved, residue, direct = coefficients(gram, center, half_width, STEPS)
    return (solution_in + combine(moved, basis), combine(residue, basis), combine(direct, basis))


def solution(mesh):
    in_specs = (
        P("gx", "gy", "gz"),
        P("gx", "gy", "gz"),
        P("gx", "gy", "gz"),
        P("gx", "gy", "gz"),
        P(),
        P(),
        P("gy", "gz"),
        P("gy", "gz"),
    )
    out_specs = (P("gx", "gy", "gz"), P("gx", "gy", "gz"), P("gx", "gy", "gz"))
    return jax.shard_map(body, mesh=mesh, in_specs=in_specs, out_specs=out_specs, check_vma=False)
```

profile of v0, /device:TPU:0, one launch (start us, length us, event | category | flops | bytes accessed | tf_op | source)
XLA Modules:
  0.0 260.0 jit_solution(15775123754584945129)
XLA Ops:
  2.2 6.3 %all-to-all-start = ((f32[4,1,1024]{2,1,0:T(1,128)}), f32[4,1,1024]{2,1,0:T(1,128)S(1)}, u32[]{:S(2)}, u32[]{:S(2)}) async-start(f32[4,1,1024]{2,1,0:T(1,128)} %reshape.745), calls=%async_computation | async-start | bytes 32768 | tf_op jit(solution)/shard_map/all_to_all | solution.py:140
  10.2 3.9 %all-to-all-done = f32[4,1,1024]{2,1,0:T(1,128)S(1)} async-done(((f32[4,1,1024]{2,1,0:T(1,128)}), f32[4,1,1024]{2,1,0:T(1,128)S(1)}, u32[]{:S(2)}, u32[]{:S(2)}) %all-to-all-start) | async-done | bytes 16416 | tf_op jit(solution)/shard_map/all_to_all | solution.py:140
  15.6 25.6 %gather_fusion = f32[4096]{0:T(1024)S(1)} fusion(f32[32,128]{1,0:T(8,128)S(1)} %reshape.660, s32[4096]{0:T(1024)S(1)} %fusion.80), kind=kCustom, calls=%fused_computation | custom fusion | bytes 65536 | tf_op jit(solution)/shard_map/jit(take_along_axis)/gather | solution.py:153
  41.3 3.4 %collective-permute-start = (f32[3,1,32,128]{3,2,1,0:T(8,128)S(1)}, f32[3,1,32,128]{3,2,1,0:T(8,128)S(1)}, u32[]{:S(2)}, u32[]{:S(2)}) collective-permute-start(f32[3,1,32,128]{3,2,1,0:T(8,128)S(1)} %get-tuple-element.320), channel_id=1, source_target_pairs={{0,16},{1,17},{2,18},{3,19},{4,20},{5,21},{6,22},{7,23},{8,24},{9,... | collective-permute-start | bytes 147464 | tf_op jit(solution)/shard_map/ppermute | solution.py:14
  44.7 1.3 collective-permute-start.1
  46.7 4.0 %collective-permute-done.1 = f32[3,1,32,128]{3,2,1,0:T(8,128)S(1)} collective-permute-done((f32[3,1,32,128]{3,2,1,0:T(8,128)S(1)}, f32[3,1,32,128]{3,2,1,0:T(8,128)S(1)}, u32[]{:S(2)}, u32[]{:S(2)}) %collective-permute-start.1) | collective-permute-done | bytes 49184 | tf_op jit(solution)/shard_map/ppermute | solution.py:17
  52.0 1.3 collective-permute-start.3
  54.0 2.8 %collective-permute-done.3 = f32[3,10,1,128]{3,2,1,0:T(1,128)S(1)} collective-permute-done((f32[3,10,1,128]{3,2,1,0:T(1,128)S(1)}, f32[3,10,1,128]{3,2,1,0:T(1,128)S(1)}, u32[]{:S(2)}, u32[]{:S(2)}) %collective-permute-start.3) | collective-permute-done | bytes 15392 | tf_op jit(solution)/shard_map/ppermute | solution.py:17
  57.4 2.6 collective-permute-start.4
  67.0 5.8 %bitcast_multiply_fusion.6 = (f32[10,34,130]{2,1,0:T(8,128)S(1)}, f32[1,10,34,130]{3,2,1,0:T(8,128)S(1)}, pred[1,10,34,130]{3,2,1,0:T(8,128)(4,1)S(1)}, pred[1,1...) fusion(f32[3,10,34,130]{3,2,1,0:T(8,128)S(1)} %pad_maximum_fusi, ...), kind=kLoop, calls=%fused_computation.85 | loop fusion | flops 1060800 | bytes 1060832 | tf_op jit(solution)/shard_map/mul | solution.py:40
  72.8 5.4 %add_add_fusion = f32[1,10,34,130]{3,2,1,0:T(8,128)S(1)} fusion(pred[1,10,34,130]{3,2,1,0:T(8,128)(4,1)S(1)} %get-tuple-element.283, pred[1,10,34,130]{3,2,1,0:T(8,128)(4,1)S(1)} %get-tuple-element.282, pred[1,10,34,130]{3,2,1,0:T(8,128)(4,1)S(1)} %get-tuple-element.281, pred[1,10,34,130]{3,2,1,0:T(8,128)(4,1)S(1)} %get-tuple-element.280, ...), kind=kLoop, calls=%fused_computation.86 | loop fusion | flops 663000 | bytes 530432 | tf_op jit(solution)/shard_map/add | solution.py:65
  79.7 1.6 collective-permute-start.6
  81.3 1.3 collective-permute-start.7
  82.8 4.2 %collective-permute-done.7 = f32[2,1,32,128]{3,2,1,0:T(8,128)S(1)} collective-permute-done((f32[2,1,32,128]{3,2,1,0:T(8,128)S(1)}, f32[2,1,32,128]{3,2,1,0:T(8,128)S(1)}, u32[]{:S(2)}, u32[]{:S(2)}) %collective-permute-start.7) | collective-permute-done | bytes 32800 | tf_op jit(solution)/shard_map/ppermute | solution.py:17
  87.1 2.4 collective-permute-start.8
  89.5 1.3 collective-permute-start.9
  90.8 3.3 %collective-permute-done.9 = f32[2,10,1,128]{3,2,1,0:T(1,128)S(1)} collective-permute-done((f32[2,10,1,128]{3,2,1,0:T(1,128)S(1)}, f32[2,10,1,128]{3,2,1,0:T(1,128)S(1)}, u32[]{:S(2)}, u32[]{:S(2)}) %collective-permute-start.9) | collective-permute-done | bytes 10272 | tf_op jit(solution)/shard_map/ppermute | solution.py:17
  94.3 4.3 %collective-permute-start.10 = (f32[2,10,34,1]{3,2,1,0:T(8,128)S(1)}, f32[2,10,34,1]{3,2,1,0:T(8,128)S(1)}, u32[]{:S(2)}, u32[]{:S(2)}) collective-permute-start(f32[2,10,34,1]{3,2,1,0:T(8,128)S(1)} %get-tuple-element.318), channel_id=1, source_target_pairs={{0,1},{1,2},{2,3},{4,5},{5,6},{6,7},{8,9},{9,10},{10,11},{12,13},{... | collective-permute-start | bytes 8168 | tf_op jit(solution)/shard_map/ppermute | solution.py:14
  98.6 1.3 collective-permute-start.11
  99.9 7.0 %collective-permute-done.10 = f32[2,10,34,1]{3,2,1,0:T(8,128)S(1)} collective-permute-done((f32[2,10,34,1]{3,2,1,0:T(8,128)S(1)}, f32[2,10,34,1]{3,2,1,0:T(8,128)S(1)}, u32[]{:S(2)}, u32[]{:S(2)}) %collective-permute-start.10) | collective-permute-done | bytes 2752 | tf_op jit(solution)/shard_map/ppermute | solution.py:14
  106.9 4.7 %collective-permute-done.11 = f32[2,10,34,1]{3,2,1,0:T(8,128)S(1)} collective-permute-done((f32[2,10,34,1]{3,2,1,0:T(8,128)S(1)}, f32[2,10,34,1]{3,2,1,0:T(8,128)S(1)}, u32[]{:S(2)}, u32[]{:S(2)}) %collective-permute-start.11) | collective-permute-done | bytes 2752 | tf_op jit(solution)/shard_map/ppermute | solution.py:17
  113.4 1.6 collective-permute-start.12
  115.0 1.3 collective-permute-start.13
  116.7 4.2 %collective-permute-done.13 = f32[2,1,32,128]{3,2,1,0:T(8,128)S(1)} collective-permute-done((f32[2,1,32,128]{3,2,1,0:T(8,128)S(1)}, f32[2,1,32,128]{3,2,1,0:T(8,128)S(1)}, u32[]{:S(2)}, u32[]{:S(2)}) %collective-permute-start.13) | collective-permute-done | bytes 32800 | tf_op jit(solution)/shard_map/ppermute | solution.py:17
  120.9 1.8 collective-permute-start.14
  122.7 1.3 collective-permute-start.15
  124.0 1.9 collective-permute-done.15
  126.2 2.4 collective-permute-start.16
  128.6 1.3 collective-permute-start.17
  129.9 7.0 %collective-permute-done.16 = f32[2,10,34,1]{3,2,1,0:T(8,128)S(1)} collective-permute-done((f32[2,10,34,1]{3,2,1,0:T(8,128)S(1)}, f32[2,10,34,1]{3,2,1,0:T(8,128)S(1)}, u32[]{:S(2)}, u32[]{:S(2)}) %collective-permute-start.16) | collective-permute-done | bytes 2752 | tf_op jit(solution)/shard_map/ppermute | solution.py:14
  136.9 4.7 %collective-permute-done.17 = f32[2,10,34,1]{3,2,1,0:T(8,128)S(1)} collective-permute-done((f32[2,10,34,1]{3,2,1,0:T(8,128)S(1)}, f32[2,10,34,1]{3,2,1,0:T(8,128)S(1)}, u32[]{:S(2)}, u32[]{:S(2)}) %collective-permute-start.17) | collective-permute-done | bytes 2752 | tf_op jit(solution)/shard_map/ppermute | solution.py:17
  144.4 1.6 collective-permute-start.18
  146.1 1.3 collective-permute-start.19
  147.5 4.2 %collective-permute-done.19 = f32[1,32,128]{2,1,0:T(8,128)S(1)} collective-permute-done((f32[1,32,128]{2,1,0:T(8,128)S(1)}, f32[1,32,128]{2,1,0:T(8,128)S(1)}, u32[]{:S(2)}, u32[]{:S(2)}) %collective-permute-start.19) | collective-permute-done | bytes 16416 | tf_op jit(solution)/shard_map/ppermute | solution.py:17
  151.7 1.5 collective-permute-start.20
  153.2 1.3 collective-permute-start.21
  156.1 1.9 dynamic-slice.147
  159.2 1.4 scatter.70
  163.1 2.5 collective-permute-start.22
  165.6 1.3 collective-permute-start.23
  167.0 3.3 %collective-permute-done.22 = f32[10,34,1]{2,1,0:T(8,128)S(1)} collective-permute-done((f32[10,34,1]{2,1,0:T(8,128)S(1)}, f32[10,34,1]{2,1,0:T(8,128)S(1)}, u32[]{:S(2)}, u32[]{:S(2)}) %collective-permute-start.22) | collective-permute-done | bytes 1392 | tf_op jit(solution)/shard_map/ppermute | solution.py:14
  170.3 4.7 %collective-permute-done.23 = f32[10,34,1]{2,1,0:T(8,128)S(1)} collective-permute-done((f32[10,34,1]{2,1,0:T(8,128)S(1)}, f32[10,34,1]{2,1,0:T(8,128)S(1)}, u32[]{:S(2)}, u32[]{:S(2)}) %collective-permute-start.23) | collective-permute-done | bytes 1392 | tf_op jit(solution)/shard_map/ppermute | solution.py:17
  178.1 1.9 stack.43
  180.0 2.9 %fusion.119 = f32[9,9]{1,0:T(8,128)S(1)} fusion(f32[9,32768]{1,0:T(8,128)S(1)} %stack.43), kind=kOutput, calls=%fused_computation.275 | convolution fusion | flops 31850496 | bytes 1179972 | tf_op jit(solution)/shard_map/dot_general | solution.py:181
  183.0 38.1 %psum.7 = f32[9,9]{1,0:T(8,128)S(1)} all-reduce(f32[9,9]{1,0:T(8,128)S(1)} %fusion.119), channel_id=1, replica_groups=mesh['gx'=2,'gy'=4,'gz'=4] {'gx','gy','gz'}, use_global_device_ids=true, to_apply=%region_3.4 | all-reduce | flops 81 | bytes 648 | tf_op jit(solution)/shard_map/psum | solution.py:182
  240.9 6.2 %multiply_add_fusion = f32[8,32,128]{2,1,0:T(8,128)} fusion(f32[8,32,128]{2,1,0:T(8,128)S(1)} %fusion.54, f32[8,32,128]{2,1,0:T(8,128)S(1)} %fusion.66, f32[8,32,128]{2,1,0:T(8,128)S(1)} %get-tuple-element.383, f32[8,32,128]{2,1,0:T(8,128)S(1)} %fusion.78, f32[8,32,128]{2,1,0:T(8,128)S(1)} %fusion.58, f32[8,32,128]{2,1,0:T(8,128)S(1)} %fusion.62, ...), kind=kLoop, calls=%fused_computation.187 | loop fusion | flops 557056 | bytes 1310756 | tf_op jit(solution)/shard_map/add | solution.py:126
  247.2 6.4 %multiply_add_fusion.1 = f32[8,32,128]{2,1,0:T(8,128)} fusion(f32[8,32,128]{2,1,0:T(8,128)S(1)} %fusion.54, f32[8,32,128]{2,1,0:T(8,128)S(1)} %fusion.66, f32[8,32,128]{2,1,0:T(8,128)S(1)} %get-tuple-element.383, f32[8,32,128]{2,1,0:T(8,128)S(1)} %fusion.78, f32[8,32,128]{2,1,0:T(8,128)S(1)} %fusion.58, f32[8,32,128]{2,1,0:T(8,128)S(1)} %fusion.62, ...), kind=kLoop, calls=%fused_computation.188 | loop fusion | flops 557056 | bytes 1310756 | tf_op jit(solution)/shard_map/add | solution.py:126
  253.6 6.4 %add_add_fusion.2 = f32[8,32,128]{2,1,0:T(8,128)} fusion(f32[8,32,128]{2,1,0:T(8,128)S(1)} %copy-done.3, f32[8,32,128]{2,1,0:T(8,128)S(1)} %fusion.54, f32[8,32,128]{2,1,0:T(8,128)S(1)} %fusion.66, f32[8,32,128]{2,1,0:T(8,128)S(1)} %get-tuple-element.383, f32[8,32,128]{2,1,0:T(8,128)S(1)} %fusion.78, f32[8,32,128]{2,1,0:T(8,128)S(1)} %fusion.58, ...), kind=kLoop, calls=%fused_computation.189 | loop fusion | flops 589824 | bytes 1441828 | tf_op jit(solution)/shard_map/add | solution.py:184
  (145 shorter events, 35.9 us)
Async XLA Ops:
  2.2 11.9 %all-to-all-start = ((f32[4,1,1024]{2,1,0:T(1,128)}), f32[4,1,1024]{2,1,0:T(1,128)S(1)}, u32[]{:S(2)}, u32[]{:S(2)}) async-start(f32[4,1,1024]{2,1,0:T(1,128)} %reshape.745), calls=%async_computation | async-start | bytes 32768 | tf_op jit(solution)/shard_map/all_to_all | solution.py:140
  15.5 25.7 %copy-start = (f32[8,32,128]{2,1,0:T(8,128)S(1)}, f32[8,32,128]{2,1,0:T(8,128)}, u32[]{:S(2)}) copy-start(f32[8,32,128]{2,1,0:T(8,128)} %param.53) | copy-start | bytes 393220
  15.5 25.7 %copy-start.4 = (s32[32,128]{1,0:T(8,128)S(1)}, s32[32,128]{1,0:T(8,128)}, u32[]{:S(2)}) copy-start(s32[32,128]{1,0:T(8,128)} %param.59) | copy-start | bytes 49156
  15.6 25.7 %copy-start.1 = (f32[8,32,128]{2,1,0:T(8,128)S(1)}, f32[8,32,128]{2,1,0:T(8,128)}, u32[]{:S(2)}) copy-start(f32[8,32,128]{2,1,0:T(8,128)} %param.54) | copy-start | bytes 393220
  15.6 30.4 %copy-start.5 = (f32[8]{0:T(128)S(1)}, f32[8]{0:T(128)}, u32[]{:S(2)}) copy-start(f32[8]{0:T(128)} %param.57) | copy-start | bytes 100
  15.6 37.7 %copy-start.6 = (f32[8]{0:T(128)S(1)}, f32[8]{0:T(128)}, u32[]{:S(2)}) copy-start(f32[8]{0:T(128)} %param.56) | copy-start | bytes 100
  41.3 5.4 %collective-permute-start = (f32[3,1,32,128]{3,2,1,0:T(8,128)S(1)}, f32[3,1,32,128]{3,2,1,0:T(8,128)S(1)}, u32[]{:S(2)}, u32[]{:S(2)}) collective-permute-start(f32[3,1,32,128]{3,2,1,0:T(8,128)S(1)} %get-tuple-element.320), channel_id=1, source_target_pairs={{0,16},{1,17},{2,18},{3,19},{4,20},{5,21},{6,22},{7,23},{8,24},{9,... | collective-permute-start | bytes 147464 | tf_op jit(solution)/shard_map/ppermute | solution.py:14
  44.7 6.0 %collective-permute-start.1 = (f32[3,1,32,128]{3,2,1,0:T(8,128)S(1)}, f32[3,1,32,128]{3,2,1,0:T(8,128)S(1)}, u32[]{:S(2)}, u32[]{:S(2)}) collective-permute-start(f32[3,1,32,128]{3,2,1,0:T(8,128)S(1)} %get-tuple-element.321), channel_id=1, source_target_pairs={{16,0},{17,1},{18,2},{19,3},{20,4},{21,5},{22,6},{23,7},{24,8},{25... | collective-permute-start | bytes 147464 | tf_op jit(solution)/shard_map/ppermute | solution.py:17
  50.7 3.3 %collective-permute-start.2 = (f32[3,10,1,128]{3,2,1,0:T(1,128)S(1)}, f32[3,10,1,128]{3,2,1,0:T(1,128)S(1)}, u32[]{:S(2)}, u32[]{:S(2)}) collective-permute-start(f32[3,10,1,128]{3,2,1,0:T(1,128)S(1)} %get-tuple-element.306), channel_id=1, source_target_pairs={{0,4},{4,8},{8,12},{1,5},{5,9},{9,13},{2,6},{6,10},{10,14},{3,7},{... | collective-permute-start | bytes 46088 | tf_op jit(solution)/shard_map/ppermute | solution.py:14
  52.0 4.8 %collective-permute-start.3 = (f32[3,10,1,128]{3,2,1,0:T(1,128)S(1)}, f32[3,10,1,128]{3,2,1,0:T(1,128)S(1)}, u32[]{:S(2)}, u32[]{:S(2)}) collective-permute-start(f32[3,10,1,128]{3,2,1,0:T(1,128)S(1)} %get-tuple-element.307), channel_id=1, source_target_pairs={{4,0},{8,4},{12,8},{5,1},{9,5},{13,9},{6,2},{10,6},{14,10},{7,3},{... | collective-permute-start | bytes 46088 | tf_op jit(solution)/shard_map/ppermute | solution.py:17
  57.4 7.8 %collective-permute-start.4 = (f32[3,10,34,1]{2,3,1,0:T(1,128)S(1)}, f32[3,10,34,1]{2,3,1,0:T(1,128)S(1)}, u32[]{:S(2)}, u32[]{:S(2)}) collective-permute-start(f32[3,10,34,1]{2,3,1,0:T(1,128)S(1)} %copy.31), channel_id=1, source_target_pairs={{0,1},{1,2},{2,3},{4,5},{5,6},{6,7},{8,9},{9,10},{10,11},{12,13},{... | collective-permute-start | bytes 12248 | tf_op jit(solution)/shard_map/ppermute | solution.py:14
  60.3 5.6 %collective-permute-start.5 = (f32[3,10,34,1]{2,3,1,0:T(1,128)S(1)}, f32[3,10,34,1]{2,3,1,0:T(1,128)S(1)}, u32[]{:S(2)}, u32[]{:S(2)}) collective-permute-start(f32[3,10,34,1]{2,3,1,0:T(1,128)S(1)} %copy.32), channel_id=1, source_target_pairs={{1,0},{2,1},{3,2},{5,4},{6,5},{7,6},{9,8},{10,9},{11,10},{13,12},{... | collective-permute-start | bytes 12248 | tf_op jit(solution)/shard_map/ppermute | solution.py:17
  79.7 3.2 %collective-permute-start.6 = (f32[2,1,32,128]{3,2,1,0:T(8,128)S(1)}, f32[2,1,32,128]{3,2,1,0:T(8,128)S(1)}, u32[]{:S(2)}, u32[]{:S(2)}) collective-permute-start(f32[2,1,32,128]{3,2,1,0:T(8,128)S(1)} %get-tuple-element.328), channel_id=1, source_target_pairs={{0,16},{1,17},{2,18},{3,19},{4,20},{5,21},{6,22},{7,23},{8,24},{9,... | collective-permute-start | bytes 98312 | tf_op jit(solution)/shard_map/ppermute | solution.py:14
  81.3 5.8 %collective-permute-start.7 = (f32[2,1,32,128]{3,2,1,0:T(8,128)S(1)}, f32[2,1,32,128]{3,2,1,0:T(8,128)S(1)}, u32[]{:S(2)}, u32[]{:S(2)}) collective-permute-start(f32[2,1,32,128]{3,2,1,0:T(8,128)S(1)} %get-tuple-element.329), channel_id=1, source_target_pairs={{16,0},{17,1},{18,2},{19,3},{20,4},{21,5},{22,6},{23,7},{24,8},{25... | collective-permute-start | bytes 98312 | tf_op jit(solution)/shard_map/ppermute | solution.py:17
  87.1 3.7 %collective-permute-start.8 = (f32[2,10,1,128]{3,2,1,0:T(1,128)S(1)}, f32[2,10,1,128]{3,2,1,0:T(1,128)S(1)}, u32[]{:S(2)}, u32[]{:S(2)}) collective-permute-start(f32[2,10,1,128]{3,2,1,0:T(1,128)S(1)} %get-tuple-element.324), channel_id=1, source_target_pairs={{0,4},{4,8},{8,12},{1,5},{5,9},{9,13},{2,6},{6,10},{10,14},{3,7},{... | collective-permute-start | bytes 30728 | tf_op jit(solution)/shard_map/ppermute | solution.py:14
  89.5 4.6 %collective-permute-start.9 = (f32[2,10,1,128]{3,2,1,0:T(1,128)S(1)}, f32[2,10,1,128]{3,2,1,0:T(1,128)S(1)}, u32[]{:S(2)}, u32[]{:S(2)}) collective-permute-start(f32[2,10,1,128]{3,2,1,0:T(1,128)S(1)} %get-tuple-element.325), channel_id=1, source_target_pairs={{4,0},{8,4},{12,8},{5,1},{9,5},{13,9},{6,2},{10,6},{14,10},{7,3},{... | collective-permute-start | bytes 30728 | tf_op jit(solution)/shard_map/ppermute | solution.py:17
  94.3 12.6 %collective-permute-start.10 = (f32[2,10,34,1]{3,2,1,0:T(8,128)S(1)}, f32[2,10,34,1]{3,2,1,0:T(8,128)S(1)}, u32[]{:S(2)}, u32[]{:S(2)}) collective-permute-start(f32[2,10,34,1]{3,2,1,0:T(8,128)S(1)} %get-tuple-element.318), channel_id=1, source_target_pairs={{0,1},{1,2},{2,3},{4,5},{5,6},{6,7},{8,9},{9,10},{10,11},{12,13},{... | collective-permute-start | bytes 8168 | tf_op jit(solution)/shard_map/ppermute | solution.py:14
  98.6 13.0 %collective-permute-start.11 = (f32[2,10,34,1]{3,2,1,0:T(8,128)S(1)}, f32[2,10,34,1]{3,2,1,0:T(8,128)S(1)}, u32[]{:S(2)}, u32[]{:S(2)}) collective-permute-start(f32[2,10,34,1]{3,2,1,0:T(8,128)S(1)} %get-tuple-element.319), channel_id=1, source_target_pairs={{1,0},{2,1},{3,2},{5,4},{6,5},{7,6},{9,8},{10,9},{11,10},{13,12},{... | collective-permute-start | bytes 8168 | tf_op jit(solution)/shard_map/ppermute | solution.py:17
  113.4 3.3 %collective-permute-start.12 = (f32[2,1,32,128]{3,2,1,0:T(8,128)S(1)}, f32[2,1,32,128]{3,2,1,0:T(8,128)S(1)}, u32[]{:S(2)}, u32[]{:S(2)}) collective-permute-start(f32[2,1,32,128]{3,2,1,0:T(8,128)S(1)} %get-tuple-element.326), channel_id=1, source_target_pairs={{0,16},{1,17},{2,18},{3,19},{4,20},{5,21},{6,22},{7,23},{8,24},{9,... | collective-permute-start | bytes 98312 | tf_op jit(solution)/shard_map/ppermute | solution.py:14
  115.0 5.9 %collective-permute-start.13 = (f32[2,1,32,128]{3,2,1,0:T(8,128)S(1)}, f32[2,1,32,128]{3,2,1,0:T(8,128)S(1)}, u32[]{:S(2)}, u32[]{:S(2)}) collective-permute-start(f32[2,1,32,128]{3,2,1,0:T(8,128)S(1)} %get-tuple-element.327), channel_id=1, source_target_pairs={{16,0},{17,1},{18,2},{19,3},{20,4},{21,5},{22,6},{23,7},{24,8},{25... | collective-permute-start | bytes 98312 | tf_op jit(solution)/shard_map/ppermute | solution.py:17
  120.9 3.1 %collective-permute-start.14 = (f32[2,10,1,128]{3,2,1,0:T(1,128)S(1)}, f32[2,10,1,128]{3,2,1,0:T(1,128)S(1)}, u32[]{:S(2)}, u32[]{:S(2)}) collective-permute-start(f32[2,10,1,128]{3,2,1,0:T(1,128)S(1)} %get-tuple-element.322), channel_id=1, source_target_pairs={{0,4},{4,8},{8,12},{1,5},{5,9},{9,13},{2,6},{6,10},{10,14},{3,7},{... | collective-permute-start | bytes 30728 | tf_op jit(solution)/shard_map/ppermute | solution.py:14
  122.7 3.2 %collective-permute-start.15 = (f32[2,10,1,128]{3,2,1,0:T(1,128)S(1)}, f32[2,10,1,128]{3,2,1,0:T(1,128)S(1)}, u32[]{:S(2)}, u32[]{:S(2)}) collective-permute-start(f32[2,10,1,128]{3,2,1,0:T(1,128)S(1)} %get-tuple-element.323), channel_id=1, source_target_pairs={{4,0},{8,4},{12,8},{5,1},{9,5},{13,9},{6,2},{10,6},{14,10},{7,3},{... | collective-permute-start | bytes 30728 | tf_op jit(solution)/shard_map/ppermute | solution.py:17
  126.2 10.7 %collective-permute-start.16 = (f32[2,10,34,1]{3,2,1,0:T(8,128)S(1)}, f32[2,10,34,1]{3,2,1,0:T(8,128)S(1)}, u32[]{:S(2)}, u32[]{:S(2)}) collective-permute-start(f32[2,10,34,1]{3,2,1,0:T(8,128)S(1)} %get-tuple-element.312), channel_id=1, source_target_pairs={{0,1},{1,2},{2,3},{4,5},{5,6},{6,7},{8,9},{9,10},{10,11},{12,13},{... | collective-permute-start | bytes 8168 | tf_op jit(solution)/shard_map/ppermute | solution.py:14
  128.6 13.0 %collective-permute-start.17 = (f32[2,10,34,1]{3,2,1,0:T(8,128)S(1)}, f32[2,10,34,1]{3,2,1,0:T(8,128)S(1)}, u32[]{:S(2)}, u32[]{:S(2)}) collective-permute-start(f32[2,10,34,1]{3,2,1,0:T(8,128)S(1)} %get-tuple-element.313), channel_id=1, source_target_pairs={{1,0},{2,1},{3,2},{5,4},{6,5},{7,6},{9,8},{10,9},{11,10},{13,12},{... | collective-permute-start | bytes 8168 | tf_op jit(solution)/shard_map/ppermute | solution.py:17
  144.1 22.8 %copy-start.10 = (f32[9,1]{0,1:T(1,128)S(1)}, f32[9,1]{0,1:T(1,128)}, u32[]{:S(2)}) copy-start(f32[9,1]{0,1:T(1,128)} %constant.804) | copy-start | bytes 112
  144.4 3.0 %collective-permute-start.18 = (f32[1,32,128]{2,1,0:T(8,128)S(1)}, f32[1,32,128]{2,1,0:T(8,128)S(1)}, u32[]{:S(2)}, u32[]{:S(2)}) collective-permute-start(f32[1,32,128]{2,1,0:T(8,128)S(1)} %get-tuple-element.334), channel_id=1, source_target_pairs={{0,16},{1,17},{2,18},{3,19},{4,20},{5,21},{6,22},{7,23},{8,24},{9,... | collective-permute-start | bytes 49160 | tf_op jit(solution)/shard_map/ppermute | solution.py:14
  146.1 5.6 %collective-permute-start.19 = (f32[1,32,128]{2,1,0:T(8,128)S(1)}, f32[1,32,128]{2,1,0:T(8,128)S(1)}, u32[]{:S(2)}, u32[]{:S(2)}) collective-permute-start(f32[1,32,128]{2,1,0:T(8,128)S(1)} %get-tuple-element.335), channel_id=1, source_target_pairs={{16,0},{17,1},{18,2},{19,3},{20,4},{21,5},{22,6},{23,7},{24,8},{25... | collective-permute-start | bytes 49160 | tf_op jit(solution)/shard_map/ppermute | solution.py:17
  151.7 11.2 %collective-permute-start.20 = (f32[10,1,128]{2,1,0:T(1,128)S(1)}, f32[10,1,128]{2,1,0:T(1,128)S(1)}, u32[]{:S(2)}, u32[]{:S(2)}) collective-permute-start(f32[10,1,128]{2,1,0:T(1,128)S(1)} %get-tuple-element.332), channel_id=1, source_target_pairs={{0,4},{4,8},{8,12},{1,5},{5,9},{9,13},{2,6},{6,10},{10,14},{3,7},{... | collective-permute-start | bytes 15368 | tf_op jit(solution)/shard_map/ppermute | solution.py:14
  153.2 9.7 %collective-permute-start.21 = (f32[10,1,128]{2,1,0:T(1,128)S(1)}, f32[10,1,128]{2,1,0:T(1,128)S(1)}, u32[]{:S(2)}, u32[]{:S(2)}) collective-permute-start(f32[10,1,128]{2,1,0:T(1,128)S(1)} %get-tuple-element.333), channel_id=1, source_target_pairs={{4,0},{8,4},{12,8},{5,1},{9,5},{13,9},{6,2},{10,6},{14,10},{7,3},{... | collective-permute-start | bytes 15368 | tf_op jit(solution)/shard_map/ppermute | solution.py:17
  163.1 7.2 %collective-permute-start.22 = (f32[10,34,1]{2,1,0:T(8,128)S(1)}, f32[10,34,1]{2,1,0:T(8,128)S(1)}, u32[]{:S(2)}, u32[]{:S(2)}) collective-permute-start(f32[10,34,1]{2,1,0:T(8,128)S(1)} %get-tuple-element.330), channel_id=1, source_target_pairs={{0,1},{1,2},{2,3},{4,5},{5,6},{6,7},{8,9},{9,10},{10,11},{12,13},{... | collective-permute-start | bytes 4088 | tf_op jit(solution)/shard_map/ppermute | solution.py:14
  165.6 9.5 %collective-permute-start.23 = (f32[10,34,1]{2,1,0:T(8,128)S(1)}, f32[10,34,1]{2,1,0:T(8,128)S(1)}, u32[]{:S(2)}, u32[]{:S(2)}) collective-permute-start(f32[10,34,1]{2,1,0:T(8,128)S(1)} %get-tuple-element.331), channel_id=1, source_target_pairs={{1,0},{2,1},{3,2},{5,4},{6,5},{7,6},{9,8},{10,9},{11,10},{13,12},{... | collective-permute-start | bytes 4088 | tf_op jit(solution)/shard_map/ppermute | solution.py:17
  175.9 1.0 copy-start.2
  180.0 41.1 %copy-start.8 = (f32[9]{0:T(128)S(1)}, f32[9]{0:T(128)}, u32[]{:S(2)}) copy-start(f32[9]{0:T(128)} %constant.686.clone.1) | copy-start | bytes 112
  180.0 41.8 %copy-start.7 = (f32[9]{0:T(128)S(1)}, f32[9]{0:T(128)}, u32[]{:S(2)}) copy-start(f32[9]{0:T(128)} %constant.661.clone.1) | copy-start | bytes 112
  180.0 41.8 %copy-start.9 = (f32[9,1]{0,1:T(1,128)S(1)}, f32[9,1]{0,1:T(1,128)}, u32[]{:S(2)}) copy-start(f32[9,1]{0,1:T(1,128)} %constant.803) | copy-start | bytes 112
  240.9 12.6 %copy-start.3 = (f32[8,32,128]{2,1,0:T(8,128)S(1)}, f32[8,32,128]{2,1,0:T(8,128)}, u32[]{:S(2)}) copy-start(f32[8,32,128]{2,1,0:T(8,128)} %param.52) | copy-start | bytes 393220
where the time goes:
time: 262 us; the launch traced here: 260 us
  waiting for transfers between devices  61.3 us (23%)
  starting transfers between devices  48.7 us (19%)
  other arithmetic  43.5 us (17%)
  local copies, waits for them, and re-layouts  42.3 us (16%)
  blocking collectives  38.1 us (15%)
  between operations  15.9 us (6%)
  matrix products  10.1 us (4%)
    ppermute x12, waiting for transfers between devices, extended(): lax.ppermute(lax.slice_in_dim(block, 0, width, axis=dim), axis, backward)  39.2 us
    psum x1, blocking collectives, body(): gram = lax.psum(partial_gram, ('gx', 'gy', 'gz'))  38.1 us
    ppermute x12, starting transfers between devices, extended(): lax.ppermute(lax.slice_in_dim(block, block.shape[dim] - width, None, axis...  26.8 us
    gather x1, local copies, waits for them, and re-layouts, body(): incoming = jnp.take_along_axis(arrived, slot, axis=1)  25.6 us
    ppermute x12, waiting for transfers between devices, extended(): lax.ppermute(lax.slice_in_dim(block, block.shape[dim] - width, None, axis...  18.2 us
    ppermute x12, starting transfers between devices, extended(): lax.ppermute(lax.slice_in_dim(block, 0, width, axis=dim), axis, backward)  15.5 us
    add x2, other arithmetic, combine(): summed = summed + weights[position] * basis[position]  12.6 us
    mul x5, other arithmetic, operate(): result = capacity * values  7.02 us
  transfers between devices with their start and end apart: 25, of which 18 were waited for; matrix products, arithmetic and copies ran while one was open for 5% of the time, Pallas kernels for 0%

commit v1 on v0

v1 whole, which is shorter than its diff:
```python
import jax
import jax.numpy as jnp
from jax import lax
from jax.experimental import pallas as pl
from jax.experimental.pallas import tpu as pltpu
from jax.sharding import PartitionSpec as P

STEPS = 4
AXES = ("gx", "gy", "gz")
MESH = pl.DeviceIdType.MESH
DIM = 2 * STEPS + 1
PAIRS = [(i, j) for i in range(DIM) for j in range(i, DIM)]
SLOT = {pair: k for k, pair in enumerate(PAIRS)}


def harmonic(a, b):
    return 2.0 * a * b / (a + b)


def times(a, b):
    return None if a is None or b is None else a * b


def plus(a, b):
    return b if a is None else a if b is None else a + b


def shift_product(p, center, half_width):
    q = [None] * DIM
    for offset, length in ((0, STEPS + 1), (STEPS + 1, STEPS)):
        for column in range(length - 1):
            entry = p[offset + column]
            if entry is None:
                continue
            q[offset + column] = plus(q[offset + column], center * entry)
            low = half_width if column == 0 else 0.5 * half_width
            q[offset + column + 1] = plus(q[offset + column + 1], low * entry)
            if column >= 1:
                q[offset + column - 1] = plus(q[offset + column - 1], 0.5 * half_width * entry)
    return q


def form(gram, a, b):
    total = None
    for i in range(DIM):
        if a[i] is None:
            continue
        row = None
        for j in range(DIM):
            row = plus(row, times(gram[i][j], b[j]))
        total = plus(total, a[i] * row)
    return total


def coefficients(gram, center, half_width):
    one = jnp.ones_like(gram[0][0])
    p = [None] * DIM
    r = [None] * DIM
    x = [None] * DIM
    p[0] = one
    r[STEPS + 1] = one
    rr = form(gram, r, r)
    for _ in range(STEPS):
        q = shift_product(p, center, half_width)
        step = rr / form(gram, p, q)
        x = [plus(x[i], times(step, p[i])) for i in range(DIM)]
        r = [plus(r[i], times(-step, q[i])) for i in range(DIM)]
        new = form(gram, r, r)
        ratio = new / rr
        p = [plus(r[i], times(ratio, p[i])) for i in range(DIM)]
        rr = new
    return x, r, p


def kernel(
    sizes, stages, cond_tab, cap_tab, sol_ref, res_ref, dir_ref, mat_ref, gas_ref, map_ref,
    sol_out, res_out, dir_out,
    basis, coef_x, coef_y, coef_z, edge_y, edge_z, diag, cond_ref,
    x_send, y_send, z_send, x_halo, y_halo, z_halo, flux_send, flux_halo, gram_send, gram_halo,
    send_sem, recv_sem, flux_ssem, flux_rsem, gram_ssem, gram_rsem,
):
    pos = {axis: lax.axis_index(axis) for axis in AXES}
    groups = sizes["gz"]
    segment = 128 // groups
    lane = lax.broadcasted_iota(jnp.int32, (8, 128), 1)
    sub = lax.broadcasted_iota(jnp.int32, (8, 128), 0)

    sides = []
    for number, axis in enumerate(AXES):
        if sizes[axis] > 1:
            sides.append((2 * number, axis, -1, pos[axis] > 0))
            sides.append((2 * number + 1, axis, 1, pos[axis] < sizes[axis] - 1))

    def zero(side):
        number, high = side // 2, side % 2
        ref = (x_halo, y_halo, z_halo)[number]
        ref[:, high] = jnp.zeros(ref.shape[:1] + ref.shape[2:], jnp.float32)

    for side in range(6):
        present = [entry[3] for entry in sides if entry[0] == side]
        if present:
            pl.when(jnp.logical_not(present[0]))(lambda side=side: zero(side))
        else:
            zero(side)

    def peers(axes):
        found = [{}]
        for axis in axes:
            found = [dict(entry, **{axis: o}) for entry in found for o in range(sizes[axis])]
        found = [entry for entry in found if any(entry.values())]
        return [
            {axis: lax.rem(pos[axis] + o, sizes[axis]) for axis, o in entry.items()} for entry in found
        ]

    def place(axes, where):
        index = 0
        for axis in axes:
            index = index * sizes[axis] + where[axis]
        return index

    barrier = pltpu.get_barrier_semaphore()
    count = 0
    for axes in stages:
        for peer in peers(axes):
            pl.semaphore_signal(barrier, inc=1, device_id=peer, device_id_type=MESH)
            count += 1

    material = mat_ref[...].reshape(32, 8, 128)
    cond = jnp.full((32, 8, 128), cond_tab[0], jnp.float32)
    cap = jnp.full((32, 8, 128), cap_tab[0], jnp.float32)
    cond_max = cond_tab[0]
    cap_max = cap_tab[0]
    cap_min = cap_tab[0]
    for m in range(1, 8):
        hit = material == m
        cond = jnp.where(hit, cond_tab[m], cond)
        cap = jnp.where(hit, cap_tab[m], cap)
        cond_max = jnp.maximum(cond_max, cond_tab[m])
        cap_max = jnp.maximum(cap_max, cap_tab[m])
        cap_min = jnp.minimum(cap_min, cap_tab[m])
    highest = cap_max + 12.0 * cond_max
    center = jnp.full((8, 128), 0.5 * (highest + cap_min), jnp.float32)
    half_width = jnp.full((8, 128), 0.5 * (highest - cap_min), jnp.float32)
    scale = 2.0 / half_width
    cond_ref[...] = cond.reshape(256, 128)

    odd = lax.rem(lane, 2) == 1
    pair_of = lax.rem(lane + 1, 128) // 2

    def copies(turn):
        result = []
        for side, axis, step, present in sides:
            number, high = side // 2, side % 2
            source = (x_send.at[turn, high], y_send.at[turn, high], z_send.at[turn])[number]
            target = (x_halo, y_halo, z_halo)[number].at[turn, 1 - high]
            result.append((side, present, pltpu.make_async_remote_copy(
                src_ref=source, dst_ref=target,
                send_sem=send_sem.at[turn, side], recv_sem=recv_sem.at[turn, side ^ 1],
                device_id={axis: pos[axis] + step}, device_id_type=MESH,
            )))
        return result

    def pack(turn, refs):
        tile = jnp.zeros((8, 128), jnp.float32)
        for f, ref in enumerate(refs):
            value = ref[...].reshape(32, 8, 128)
            x_send[turn, 0, f] = value[0:4]
            x_send[turn, 1, f] = value[28:32]
            y_send[turn, 0, f] = ref[pl.ds(0, 8, stride=32), :]
            y_send[turn, 1, f] = ref[pl.ds(31, 8, stride=32), :]
            for g in range(32):
                k = 32 * f + g
                moved = pltpu.roll(value[g], 2 * k, axis=1) if k else value[g]
                tile = jnp.where(pair_of == k, moved, tile)
        z_send[turn] = tile

    def start(turn):
        for side, present, copy in copies(turn):
            pl.when(present)(copy.start)

    def wait(turn):
        for side, axis, step, present in sides:
            number, high = side // 2, side % 2
            target = (x_halo, y_halo, z_halo)[number].at[turn, high]
            copy = pltpu.make_async_remote_copy(
                src_ref=target, dst_ref=target,
                send_sem=send_sem.at[turn, side], recv_sem=recv_sem.at[turn, side],
                device_id={axis: pos[axis] + step}, device_id_type=MESH,
            )
            pl.when(present)(copy.wait_recv)

    def halo(turn, f, mixed):
        rows = []
        for high in range(2):
            rows.append(jnp.stack([
                jnp.broadcast_to(y_halo[turn, high, f, pl.ds(x, 1), :], (8, 128)) for x in range(8)
            ]))
        columns = []
        for g in range(32):
            k = 32 * f + g
            columns.append(pltpu.roll(mixed, 128 - 2 * k, axis=1) if k else mixed)
        return x_halo[turn, 0, f], x_halo[turn, 1, f], rows[0], rows[1], jnp.stack(columns)

    def mix(turn):
        low = pltpu.roll(z_halo[turn, 0], 1, axis=1)
        high = pltpu.roll(z_halo[turn, 1], 127, axis=1)
        return jnp.where(odd, high, low)

    def around(v):
        zeros4 = jnp.zeros((4, 8, 128), jnp.float32)
        xl = jnp.concatenate([zeros4, v[:28]], axis=0)
        xh = jnp.concatenate([v[4:], zeros4], axis=0)
        zeros1 = jnp.zeros((8, 1, 8, 128), jnp.float32)
        down = pltpu.roll(v, 1, axis=1)
        down4 = down.reshape(8, 4, 8, 128)
        before = jnp.concatenate([zeros1, down4[:, :3]], axis=1).reshape(32, 8, 128)
        yl = jnp.where(sub == 0, before, down)
        up = pltpu.roll(v, 7, axis=1)
        up4 = up.reshape(8, 4, 8, 128)
        after = jnp.concatenate([up4[:, 1:], zeros1], axis=1).reshape(32, 8, 128)
        yh = jnp.where(sub == 7, after, up)
        return xl, xh, yl, yh, pltpu.roll(v, 1, axis=2), pltpu.roll(v, 127, axis=2)

    def interior(v):
        xl, xh, yl, yh, zl, zh = around(v)
        return (
            diag[...] * v - coef_x[0:32] * xl - coef_x[4:36] * xh
            - coef_y[0] * yl - coef_y[1] * yh - coef_z[0] * zl - coef_z[1] * zh
        )

    def border(acc, turn, f, mixed):
        xl, xh, yl, yh, zz = halo(turn, f, mixed)
        acc = acc - edge_z[...] * zz
        acc4 = acc.reshape(8, 4, 8, 128)
        acc = jnp.concatenate([
            (acc4[:, 0] - edge_y[0] * yl)[:, None],
            acc4[:, 1:3],
            (acc4[:, 3] - edge_y[1] * yh)[:, None],
        ], axis=1).reshape(32, 8, 128)
        return jnp.concatenate([
            acc[0:4] - coef_x[0:4] * xl, acc[4:28], acc[28:32] - coef_x[32:36] * xh
        ], axis=0)

    def term(i):
        return basis[i].reshape(32, 8, 128)

    def gram_part(total, pairs):
        for i, j in pairs:
            value = jnp.sum(term(i) * term(j), axis=0)
            value = jnp.sum(value, axis=1, keepdims=True)
            total = jnp.where(lane == SLOT[(i, j)], value, total)
        return total

    basis[0] = dir_ref[...].reshape(256, 128)
    pack(0, [basis.at[0], cond_ref])

    for t in range(groups):
        tile = jnp.zeros((8, 128), jnp.float32)
        for a in range(4):
            amount = ((a - t) * segment) % 128
            rows = gas_ref[8 * a:8 * a + 8, :]
            moved = pltpu.roll(rows, amount, axis=1) if amount else rows
            tile = jnp.where(lane // segment == a, moved, tile)
        flux_send[t] = tile
    pl.semaphore_wait(barrier, count)
    start(0)
    flux_copies = []
    for o in range(1, groups):
        t = lax.rem(pos["gz"] + o, groups)
        flux_copies.append(pltpu.make_async_remote_copy(
            src_ref=flux_send.at[t], dst_ref=flux_halo.at[pos["gz"]],
            send_sem=flux_ssem.at[t], recv_sem=flux_rsem.at[pos["gz"]],
            device_id={"gz": t}, device_id_type=MESH,
        ))
        flux_copies[-1].start()
    flux_halo[pos["gz"]] = flux_send[pos["gz"]]

    xl, xh, yl, yh, zl, zh = around(cond)
    wide = scale[None]
    kx = harmonic(xl, cond) * wide
    coef_x[4:32] = kx[4:32]
    kyl = harmonic(yl, cond) * wide
    kyh = harmonic(yh, cond) * wide
    kzl = jnp.where(lane == 0, 0.0, harmonic(zl, cond) * wide)
    kzh = jnp.where(lane == 127, 0.0, harmonic(zh, cond) * wide)
    coef_y[0] = kyl
    coef_y[1] = kyh
    coef_z[0] = kzl
    coef_z[1] = kzh
    diag_in = (cap - center) * wide + kyl + kyh + kzl + kzh
    total = gram_part(jnp.zeros((8, 128), jnp.float32), [(0, 0)])

    for o in range(1, groups):
        t = lax.rem(pos["gz"] + o, groups)
        pltpu.make_async_remote_copy(
            src_ref=flux_halo.at[t], dst_ref=flux_halo.at[t],
            send_sem=flux_ssem.at[t], recv_sem=flux_rsem.at[t],
            device_id={"gz": t}, device_id_type=MESH,
        ).wait_recv()
    is_top = pos["gx"] == sizes["gx"] - 1
    basis[STEPS + 1] = res_ref[...].reshape(256, 128)
    for a in range(4):
        wanted = map_ref[8 * a:8 * a + 8, :]
        holder = wanted // 128
        index = lax.rem(wanted, 128) + (a - pos["gz"]) * segment
        incoming = jnp.zeros((8, 128), jnp.float32)
        for q in range(groups):
            found = jnp.take_along_axis(flux_halo[q], index, axis=1)
            incoming = jnp.where(holder == q, found, incoming)
        rows = slice(224 + 8 * a, 232 + 8 * a)
        basis[STEPS + 1, rows, :] = res_ref[7, 8 * a:8 * a + 8, :] + jnp.where(is_top, incoming, 0.0)

    wait(0)
    mixed = mix(0)
    xl, xh, yl, yh, zz = halo(0, 1, mixed)
    cond4 = cond.reshape(8, 4, 8, 128)
    coef_x[0:4] = harmonic(xl, cond[0:4]) * wide
    coef_x[32:36] = harmonic(cond[28:32], xh) * wide
    eyl = jnp.where(sub == 0, harmonic(yl, cond4[:, 0]) * wide, 0.0)
    eyh = jnp.where(sub == 7, harmonic(yh, cond4[:, 3]) * wide, 0.0)
    edge_y[0] = eyl
    edge_y[1] = eyh
    ends = jnp.logical_or(lane == 0, lane == 127)
    beside = jnp.where(ends, zz, 0.0)
    ez = harmonic(beside, cond) * wide
    edge_z[...] = ez
    diag_in = diag_in + coef_x[0:32] + coef_x[4:36] + ez
    diag4 = diag_in.reshape(8, 4, 8, 128)
    diag[...] = jnp.concatenate([
        (diag4[:, 0] + eyl)[:, None], diag4[:, 1:3], (diag4[:, 3] + eyh)[:, None]
    ], axis=1).reshape(32, 8, 128)
    basis[1] = (0.5 * border(interior(term(0)), 0, 0, mixed)).reshape(256, 128)

    done = [0]
    for turn in range(1, STEPS):
        d, s = turn, STEPS + turn
        pack(turn, [basis.at[d], basis.at[s]])
        start(turn)
        d_next = interior(term(d))
        s_next = interior(term(s))
        fresh = [d, s]
        done = done + fresh
        total = gram_part(total, [
            (i, j) for i, j in PAIRS if i in done and j in done and (i in fresh or j in fresh)
        ])
        wait(turn)
        mixed = mix(turn)
        d_next = border(d_next, turn, 0, mixed) - term(d - 1)
        s_next = border(s_next, turn, 1, mixed)
        s_next = 0.5 * s_next if turn == 1 else s_next - term(s - 1)
        basis[d + 1] = d_next.reshape(256, 128)
        basis[s + 1] = s_next.reshape(256, 128)

    fresh = [STEPS, 2 * STEPS]
    total = gram_part(total, [(i, j) for i, j in PAIRS if i in fresh or j in fresh])
    row = jnp.sum(total, axis=0, keepdims=True)
    base = 0
    gram_copies = []
    for stage, axes in enumerate(stages):
        members = 1
        for axis in axes:
            members *= sizes[axis]
        own = base + place(axes, pos)
        gram_send[stage] = row
        gram_halo[own] = row
        for peer in peers(axes):
            other = base + place(axes, peer)
            copy = pltpu.make_async_remote_copy(
                src_ref=gram_send.at[stage], dst_ref=gram_halo.at[own],
                send_sem=gram_ssem.at[other], recv_sem=gram_rsem.at[own],
                device_id=peer, device_id_type=MESH,
            )
            copy.start()
            gram_copies.append(copy)
        for peer in peers(axes):
            other = base + place(axes, peer)
            pltpu.make_async_remote_copy(
                src_ref=gram_halo.at[other], dst_ref=gram_halo.at[other],
                send_sem=gram_ssem.at[other], recv_sem=gram_rsem.at[other],
                device_id=peer, device_id_type=MESH,
            ).wait_recv()
        row = jnp.sum(gram_halo[base:base + members], axis=0)
        base += members

    gram = [[None] * DIM for _ in range(DIM)]
    for (i, j), k in SLOT.items():
        gram[i][j] = gram[j][i] = jnp.broadcast_to(row[:, k:k + 1], (8, 128))
    moved, residue, direct = coefficients(gram, center, half_width)

    for weights, out in ((moved, sol_out), (residue, res_out), (direct, dir_out)):
        summed = None
        for i in range(DIM):
            if weights[i] is not None:
                summed = plus(summed, weights[i][None] * term(i))
        if out is sol_out:
            summed = sol_ref[...].reshape(32, 8, 128) + summed
        out[...] = summed.reshape(8, 32, 128)

    for turn in range(STEPS):
        for side, present, copy in copies(turn):
            pl.when(present)(copy.wait_send)
    for copy in flux_copies + gram_copies:
        copy.wait_send()


def solution(mesh):
    sizes = {axis: mesh.shape[axis] for axis in AXES}
    total = sizes["gx"] * sizes["gy"] * sizes["gz"]
    stages = [AXES] if total <= 64 else [(axis,) for axis in AXES]
    rows = 0
    for axes in stages:
        members = 1
        for axis in axes:
            members *= sizes[axis]
        rows += members

    def body(sol, res, direction, material, cond_table, cap_table, gas, supply):
        vmem = pl.BlockSpec(memory_space=pltpu.VMEM)
        smem = pl.BlockSpec(memory_space=pltpu.SMEM)
        f32 = jnp.float32
        block = jax.ShapeDtypeStruct(sol.shape, f32)
        return pl.pallas_call(
            lambda *refs: kernel(sizes, stages, *refs),
            out_shape=(block, block, block),
            in_specs=[smem, smem] + [vmem] * 6,
            out_specs=(vmem, vmem, vmem),
            scratch_shapes=[
                pltpu.VMEM((DIM, 256, 128), f32),
                pltpu.VMEM((36, 8, 128), f32),
                pltpu.VMEM((2, 32, 8, 128), f32),
                pltpu.VMEM((2, 32, 8, 128), f32),
                pltpu.VMEM((2, 8, 8, 128), f32),
                pltpu.VMEM((32, 8, 128), f32),
                pltpu.VMEM((32, 8, 128), f32),
                pltpu.VMEM((256, 128), f32),
                pltpu.VMEM((STEPS, 2, 2, 4, 8, 128), f32),
                pltpu.VMEM((STEPS, 2, 2, 8, 128), f32),
                pltpu.VMEM((STEPS, 8, 128), f32),
                pltpu.VMEM((STEPS, 2, 2, 4, 8, 128), f32),
                pltpu.VMEM((STEPS, 2, 2, 8, 128), f32),
                pltpu.VMEM((STEPS, 2, 8, 128), f32),
                pltpu.VMEM((sizes["gz"], 8, 128), f32),
                pltpu.VMEM((sizes["gz"], 8, 128), f32),
                pltpu.VMEM((len(stages), 1, 128), f32),
                pltpu.VMEM((rows, 1, 128), f32),
                pltpu.SemaphoreType.DMA((STEPS, 6)),
                pltpu.SemaphoreType.DMA((STEPS, 6)),
                pltpu.SemaphoreType.DMA((sizes["gz"],)),
                pltpu.SemaphoreType.DMA((sizes["gz"],)),
                pltpu.SemaphoreType.DMA((rows,)),
                pltpu.SemaphoreType.DMA((rows,)),
            ],
            compiler_params=pltpu.CompilerParams(
                collective_id=0, has_side_effects=True, vmem_limit_bytes=32 * 1024 * 1024
            ),
            cost_estimate=pl.CostEstimate(flops=10**7, bytes_accessed=10**6, transcendentals=0),
        )(cond_table, cap_table, sol, res, direction, material, gas, supply)

    spec = P("gx", "gy", "gz")
    in_specs = (spec, spec, spec, spec, P(), P(), P("gy", "gz"), P("gy", "gz"))
    return jax.shard_map(
        body, mesh=mesh, in_specs=in_specs, out_specs=(spec, spec, spec), check_vma=False
    )
```

time: 262 us -> 36.8 us (0.14)
  waiting for transfers between devices: 61.3 us -> 0 us
  starting transfers between devices: 48.7 us -> 0 us
  other arithmetic: 43.5 us -> 0 us
  blocking collectives: 38.1 us -> 0 us
  local copies, waits for them, and re-layouts: 42.3 us -> 8.32 us
  Pallas kernels: 0 us -> 27.5 us
  between operations: 15.9 us -> 0.66 us
  matrix products: 10.1 us -> 0 us
    ppermute x24 -> x0, waiting for transfers between devices: 57.4 us -> none  [the longest x12 39.2 us: extended(): lax.ppermute(lax.slice_in_dim(block, 0, width, axis=dim), axis, backward)]
    ppermute x24 -> x0, starting transfers between devices: 42.3 us -> none  [the longest x12 26.8 us: extended(): lax.ppermute(lax.slice_in_dim(block, block.shape[dim] - width, None, axis...]
    psum x1 -> x0, blocking collectives: 38.1 us -> none  [body(): gram = lax.psum(partial_gram, ('gx', 'gy', 'gz'))]
    pallas_call x0 -> x1, Pallas kernels: none -> 27.5 us  [body(): pl.pallas_call(lambda *refs: kernel(sizes, stages, *refs), out_shape=(blo...]
    gather x1 -> x0, local copies, waits for them, and re-layouts: 25.6 us -> none  [body(): incoming = jnp.take_along_axis(arrived, slot, axis=1)]
    add x8 -> x0, other arithmetic: 24.4 us -> none  [the longest x2 12.6 us: combine(): summed = summed + weights[position] * basis[position]]
    dot_general x14 -> x0, matrix products: 10.1 us -> none  [the longest x9 6.67 us: gram_product(): jnp.dot(gram, second_vec, precision=highest_prec)]
    mul x20 -> x0, other arithmetic: 9.94 us -> none  [the longest x5 7.02 us: operate(): result = capacity * values]
  transfers between devices with their start and end apart: 25 -> 0, of which waited for: 18 -> 0; matrix products, arithmetic and copies ran while one was open for 5% -> 0% of each run, Pallas kernels for 0% -> 0%
where the time goes in v1:
time: 36.8 us; the launch traced here: 36.5 us
  Pallas kernels  27.5 us (75%)
  local copies, waits for them, and re-layouts  8.32 us (23%)
  between operations  0.66 us (2%)
    pallas_call x1, Pallas kernels, body(): pl.pallas_call(lambda *refs: kernel(sizes, stages, *refs), out_shape=(blo...  27.5 us
    unnamed x19, local copies, waits for them, and re-layouts  8.32 us

profile of v1, /device:TPU:0, one launch (start us, length us, event | category | flops | bytes accessed | tf_op | source)
XLA Modules:
  0.0 36.5 jit_solution(1698977633942176608)
XLA Ops:
  0.6 0.0 copy-start
  0.6 0.9 %copy-done = f32[8,32,128]{2,1,0:T(8,128)S(1)} copy-done((f32[8,32,128]{2,1,0:T(8,128)S(1)}, f32[8,32,128]{2,1,0:T(8,128)}, u32[]{:S(2)}) %copy-start) | copy-done | bytes 131096
  1.5 0.0 copy-start.1
  1.5 0.9 %copy-done.1 = f32[8,32,128]{2,1,0:T(8,128)S(1)} copy-done((f32[8,32,128]{2,1,0:T(8,128)S(1)}, f32[8,32,128]{2,1,0:T(8,128)}, u32[]{:S(2)}) %copy-start.1) | copy-done | bytes 131096
  2.4 0.0 copy-start.2
  2.4 0.9 %copy-done.2 = f32[8,32,128]{2,1,0:T(8,128)S(1)} copy-done((f32[8,32,128]{2,1,0:T(8,128)S(1)}, f32[8,32,128]{2,1,0:T(8,128)}, u32[]{:S(2)}) %copy-start.2) | copy-done | bytes 131096
  3.3 0.0 copy-start.3
  3.4 0.9 %copy-done.3 = s32[8,32,128]{2,1,0:T(8,128)S(1)} copy-done((s32[8,32,128]{2,1,0:T(8,128)S(1)}, s32[8,32,128]{2,1,0:T(8,128)}, u32[]{:S(2)}) %copy-start.3) | copy-done | bytes 131096
  4.3 0.0 copy-start.4
  4.3 0.7 %copy-done.4 = f32[32,128]{1,0:T(8,128)S(1)} copy-done((f32[32,128]{1,0:T(8,128)S(1)}, f32[32,128]{1,0:T(8,128)}, u32[]{:S(2)}) %copy-start.4) | copy-done | bytes 16408
  5.0 0.0 copy-start.5
  5.0 0.7 %copy-done.5 = s32[32,128]{1,0:T(8,128)S(1)} copy-done((s32[32,128]{1,0:T(8,128)S(1)}, s32[32,128]{1,0:T(8,128)}, u32[]{:S(2)}) %copy-start.5) | copy-done | bytes 16408
  5.7 0.0 copy-start.6
  5.7 0.7 %copy-done.6 = f32[8]{0:T(128)S(1)} copy-done((f32[8]{0:T(128)S(1)}, f32[8]{0:T(128)}, u32[]{:S(2)}) %copy-start.6) | copy-done | bytes 56
  6.3 0.0 copy-start.7
  6.3 0.7 %copy-done.7 = f32[8]{0:T(128)S(1)} copy-done((f32[8]{0:T(128)S(1)}, f32[8]{0:T(128)}, u32[]{:S(2)}) %copy-start.7) | copy-done | bytes 56
  7.0 27.5 %shard_map.103 = (f32[8,32,128]{2,1,0:T(8,128)S(1)}, f32[8,32,128]{2,1,0:T(8,128)S(1)}, f32[8,32,128]{2,1,0:T(8,128)S(1)}) custom-call(f32[8]{0:T(128)S(1)} %copy-done.6, f32[8]{0:T(128)S(1)} %copy-done.7, f32[8,32,128]{2,1,0:T(8,128)S(1)} %copy-done, f32[8,32,128]{2,1,0:T(8,128)S(1)} %copy-done.1, f32[8,32,128]{2,1,0:T(8,128)S(1)} %copy-done.2, ...), custom_call_target="tpu_custom_call" | custom-call | flops 10000000 | bytes 1000000 | tf_op jit(solution)/shard_map/pallas_call | solution.py:422
  34.5 0.7 %copy.14 = f32[8,32,128]{2,1,0:T(8,128)} copy(f32[8,32,128]{2,1,0:T(8,128)S(1)} %get-tuple-element.6) | data formatting | bytes 262144
  35.1 0.7 %copy.15 = f32[8,32,128]{2,1,0:T(8,128)} copy(f32[8,32,128]{2,1,0:T(8,128)S(1)} %get-tuple-element.7) | data formatting | bytes 262144
  35.8 0.7 %copy.16 = f32[8,32,128]{2,1,0:T(8,128)} copy(f32[8,32,128]{2,1,0:T(8,128)S(1)} %get-tuple-element.8) | data formatting | bytes 262144
Async XLA Ops:
  0.6 0.9 %copy-start = (f32[8,32,128]{2,1,0:T(8,128)S(1)}, f32[8,32,128]{2,1,0:T(8,128)}, u32[]{:S(2)}) copy-start(f32[8,32,128]{2,1,0:T(8,128)} %refs_2_.1) | copy-start | bytes 393220
  1.5 0.9 %copy-start.1 = (f32[8,32,128]{2,1,0:T(8,128)S(1)}, f32[8,32,128]{2,1,0:T(8,128)}, u32[]{:S(2)}) copy-start(f32[8,32,128]{2,1,0:T(8,128)} %refs_3_.1) | copy-start | bytes 393220
  2.4 0.9 %copy-start.2 = (f32[8,32,128]{2,1,0:T(8,128)S(1)}, f32[8,32,128]{2,1,0:T(8,128)}, u32[]{:S(2)}) copy-start(f32[8,32,128]{2,1,0:T(8,128)} %refs_4_.1) | copy-start | bytes 393220
  3.3 0.9 %copy-start.3 = (s32[8,32,128]{2,1,0:T(8,128)S(1)}, s32[8,32,128]{2,1,0:T(8,128)}, u32[]{:S(2)}) copy-start(s32[8,32,128]{2,1,0:T(8,128)} %refs_5_.1) | copy-start | bytes 393220
  4.3 0.7 %copy-start.4 = (f32[32,128]{1,0:T(8,128)S(1)}, f32[32,128]{1,0:T(8,128)}, u32[]{:S(2)}) copy-start(f32[32,128]{1,0:T(8,128)} %refs_6_.1) | copy-start | bytes 49156
  5.0 0.7 %copy-start.5 = (s32[32,128]{1,0:T(8,128)S(1)}, s32[32,128]{1,0:T(8,128)}, u32[]{:S(2)}) copy-start(s32[32,128]{1,0:T(8,128)} %refs_7_.1) | copy-start | bytes 49156
  5.7 0.7 %copy-start.6 = (f32[8]{0:T(128)S(1)}, f32[8]{0:T(128)}, u32[]{:S(2)}) copy-start(f32[8]{0:T(128)} %refs_0_.1) | copy-start | bytes 100
  6.3 0.7 %copy-start.7 = (f32[8]{0:T(128)S(1)}, f32[8]{0:T(128)}, u32[]{:S(2)}) copy-start(f32[8]{0:T(128)} %refs_1_.1) | copy-start | bytes 100

commit v2 on v1

--- a/solution.py
+++ b/solution.py
@@ -6,6 +6,7 @@
 from jax.sharding import PartitionSpec as P
 
 STEPS = 4
+VMEM = 63 * 1024 * 1024
 AXES = ("gx", "gy", "gz")
 MESH = pl.DeviceIdType.MESH
 DIM = 2 * STEPS + 1
@@ -15,6 +16,12 @@
 
 def harmonic(a, b):
     return 2.0 * a * b / (a + b)
+
+
+def tree(parts):
+    while len(parts) > 1:
+        parts = [sum(parts[k:k + 2][1:], parts[k]) for k in range(0, len(parts), 2)]
+    return parts[0]
 
 
 def times(a, b):
@@ -73,12 +80,19 @@
 
 
 def kernel(
-    sizes, stages, cond_tab, cap_tab, sol_ref, res_ref, dir_ref, mat_ref, gas_ref, map_ref,
+    sizes, stages, cond_in, cap_in, sol_in, res_in, dir_in, mat_in, gas_in, map_in,
     sol_out, res_out, dir_out,
-    basis, coef_x, coef_y, coef_z, edge_y, edge_z, diag, cond_ref,
+    basis, held, store_sem, cond_tab, cap_tab, res_ref, mat_ref, gas_ref, map_ref,
+    coef_x, coef_y, coef_z, edge_y, edge_z, diag, cond_ref,
     x_send, y_send, z_send, x_halo, y_halo, z_halo, flux_send, flux_halo, gram_send, gram_halo,
-    send_sem, recv_sem, flux_ssem, flux_rsem, gram_ssem, gram_rsem,
+    send_sem, recv_sem, flux_ssem, flux_rsem, gram_ssem, gram_rsem, load_sem,
 ):
+    loads = []
+    for source, target in (
+        (dir_in, basis.at[0]), (mat_in, mat_ref), (cond_in, cond_tab), (cap_in, cap_tab),
+        (gas_in, gas_ref), (res_in, res_ref), (map_in, map_ref), (sol_in, held.at[0]),
+    ):
+        loads.append(pltpu.make_async_copy(source, target, load_sem.at[len(loads)]))
     pos = {axis: lax.axis_index(axis) for axis in AXES}
     groups = sizes["gz"]
     segment = 128 // groups
@@ -120,12 +134,16 @@
 
     barrier = pltpu.get_barrier_semaphore()
     count = 0
-    for axes in stages:
-        for peer in peers(axes):
+    for axis in AXES:
+        for peer in peers((axis,)):
             pl.semaphore_signal(barrier, inc=1, device_id=peer, device_id_type=MESH)
             count += 1
-
-    material = mat_ref[...].reshape(32, 8, 128)
+    for load in loads:
+        load.start()
+    for load in loads[:4]:
+        load.wait()
+
+    material = mat_ref[...]
     cond = jnp.full((32, 8, 128), cond_tab[0], jnp.float32)
     cap = jnp.full((32, 8, 128), cap_tab[0], jnp.float32)
     cond_max = cond_tab[0]
@@ -141,7 +159,6 @@
     highest = cap_max + 12.0 * cond_max
     center = jnp.full((8, 128), 0.5 * (highest + cap_min), jnp.float32)
     half_width = jnp.full((8, 128), 0.5 * (highest - cap_min), jnp.float32)
-    scale = 2.0 / half_width
     cond_ref[...] = cond.reshape(256, 128)
 
     odd = lax.rem(lane, 2) == 1
@@ -246,14 +263,15 @@
 
     def gram_part(total, pairs):
         for i, j in pairs:
-            value = jnp.sum(term(i) * term(j), axis=0)
+            product = term(i) * term(j)
+            value = tree([tree([product[8 * a + g] for a in range(4)]) for g in range(8)])
             value = jnp.sum(value, axis=1, keepdims=True)
             total = jnp.where(lane == SLOT[(i, j)], value, total)
         return total
 
-    basis[0] = dir_ref[...].reshape(256, 128)
     pack(0, [basis.at[0], cond_ref])
 
+    loads[4].wait()
     for t in range(groups):
         tile = jnp.zeros((8, 128), jnp.float32)
         for a in range(4):
@@ -276,18 +294,17 @@
     flux_halo[pos["gz"]] = flux_send[pos["gz"]]
 
     xl, xh, yl, yh, zl, zh = around(cond)
-    wide = scale[None]
-    kx = harmonic(xl, cond) * wide
+    kx = harmonic(xl, cond)
     coef_x[4:32] = kx[4:32]
-    kyl = harmonic(yl, cond) * wide
-    kyh = harmonic(yh, cond) * wide
-    kzl = jnp.where(lane == 0, 0.0, harmonic(zl, cond) * wide)
-    kzh = jnp.where(lane == 127, 0.0, harmonic(zh, cond) * wide)
+    kyl = harmonic(yl, cond)
+    kyh = harmonic(yh, cond)
+    kzl = jnp.where(lane == 0, 0.0, harmonic(zl, cond))
+    kzh = jnp.where(lane == 127, 0.0, harmonic(zh, cond))
     coef_y[0] = kyl
     coef_y[1] = kyh
     coef_z[0] = kzl
     coef_z[1] = kzh
-    diag_in = (cap - center) * wide + kyl + kyh + kzl + kzh
+    diag_in = (cap - center) + kyl + kyh + kzl + kzh
     total = gram_part(jnp.zeros((8, 128), jnp.float32), [(0, 0)])
 
     for o in range(1, groups):
@@ -298,7 +315,9 @@
             device_id={"gz": t}, device_id_type=MESH,
         ).wait_recv()
     is_top = pos["gx"] == sizes["gx"] - 1
-    basis[STEPS + 1] = res_ref[...].reshape(256, 128)
+    loads[5].wait()
+    loads[6].wait()
+    basis[STEPS + 1] = res_ref[...]
     for a in range(4):
         wanted = map_ref[8 * a:8 * a + 8, :]
         holder = wanted // 128
@@ -308,28 +327,28 @@
             found = jnp.take_along_axis(flux_halo[q], index, axis=1)
             incoming = jnp.where(holder == q, found, incoming)
         rows = slice(224 + 8 * a, 232 + 8 * a)
-        basis[STEPS + 1, rows, :] = res_ref[7, 8 * a:8 * a + 8, :] + jnp.where(is_top, incoming, 0.0)
+        basis[STEPS + 1, rows, :] = res_ref[rows, :] + jnp.where(is_top, incoming, 0.0)
 
     wait(0)
     mixed = mix(0)
     xl, xh, yl, yh, zz = halo(0, 1, mixed)
     cond4 = cond.reshape(8, 4, 8, 128)
-    coef_x[0:4] = harmonic(xl, cond[0:4]) * wide
-    coef_x[32:36] = harmonic(cond[28:32], xh) * wide
-    eyl = jnp.where(sub == 0, harmonic(yl, cond4[:, 0]) * wide, 0.0)
-    eyh = jnp.where(sub == 7, harmonic(yh, cond4[:, 3]) * wide, 0.0)
+    coef_x[0:4] = harmonic(xl, cond[0:4])
+    coef_x[32:36] = harmonic(cond[28:32], xh)
+    eyl = jnp.where(sub == 0, harmonic(yl, cond4[:, 0]), 0.0)
+    eyh = jnp.where(sub == 7, harmonic(yh, cond4[:, 3]), 0.0)
     edge_y[0] = eyl
     edge_y[1] = eyh
     ends = jnp.logical_or(lane == 0, lane == 127)
     beside = jnp.where(ends, zz, 0.0)
-    ez = harmonic(beside, cond) * wide
+    ez = harmonic(beside, cond)
     edge_z[...] = ez
     diag_in = diag_in + coef_x[0:32] + coef_x[4:36] + ez
     diag4 = diag_in.reshape(8, 4, 8, 128)
     diag[...] = jnp.concatenate([
         (diag4[:, 0] + eyl)[:, None], diag4[:, 1:3], (diag4[:, 3] + eyh)[:, None]
     ], axis=1).reshape(32, 8, 128)
-    basis[1] = (0.5 * border(interior(term(0)), 0, 0, mixed)).reshape(256, 128)
+    basis[1] = (border(interior(term(0)), 0, 0, mixed) / half_width).reshape(256, 128)
 
     done = [0]
     for turn in range(1, STEPS):
@@ -345,9 +364,9 @@
         ])
         wait(turn)
         mixed = mix(turn)
-        d_next = border(d_next, turn, 0, mixed) - term(d - 1)
-        s_next = border(s_next, turn, 1, mixed)
-        s_next = 0.5 * s_next if turn == 1 else s_next - term(s - 1)
+        d_next = 2.0 * (border(d_next, turn, 0, mixed) / half_width) - term(d - 1)
+        s_next = border(s_next, turn, 1, mixed) / half_width
+        s_next = s_next if turn == 1 else 2.0 * s_next - term(s - 1)
         basis[d + 1] = d_next.reshape(256, 128)
         basis[s + 1] = s_next.reshape(256, 128)
 
@@ -379,7 +398,7 @@
                 send_sem=gram_ssem.at[other], recv_sem=gram_rsem.at[other],
                 device_id=peer, device_id_type=MESH,
             ).wait_recv()
-        row = jnp.sum(gram_halo[base:base + members], axis=0)
+        row = tree([gram_halo[base + member] for member in range(members)])
         base += members
 
     gram = [[None] * DIM for _ in range(DIM)]
@@ -387,20 +406,40 @@
         gram[i][j] = gram[j][i] = jnp.broadcast_to(row[:, k:k + 1], (8, 128))
     moved, residue, direct = coefficients(gram, center, half_width)
 
-    for weights, out in ((moved, sol_out), (residue, res_out), (direct, dir_out)):
-        summed = None
+    stores = []
+    loads[7].wait()
+    for number, weights, out in ((1, residue, res_out), (2, direct, dir_out), (0, moved, sol_out)):
+        summed = held[0] if number == 0 else None
         for i in range(DIM):
             if weights[i] is not None:
                 summed = plus(summed, weights[i][None] * term(i))
-        if out is sol_out:
-            summed = sol_ref[...].reshape(32, 8, 128) + summed
-        out[...] = summed.reshape(8, 32, 128)
+        held[number] = summed
+        stores.append(pltpu.make_async_copy(held.at[number], out, store_sem.at[number]))
+        stores[-1].start()
 
     for turn in range(STEPS):
         for side, present, copy in copies(turn):
             pl.when(present)(copy.wait_send)
     for copy in flux_copies + gram_copies:
         copy.wait_send()
+    for store in stores:
+        store.wait()
+
+
+def finish(res_in, dir_in, sol_in, res_out, dir_out, sol_out, held, load_sem, store_sem):
+    loads = []
+    for source in (res_in, dir_in, sol_in):
+        k = len(loads)
+        loads.append(pltpu.make_async_copy(source, held.at[k], load_sem.at[k]))
+        loads[k].start()
+    stores = []
+    for target in (res_out, dir_out, sol_out):
+        k = len(stores)
+        loads[k].wait()
+        stores.append(pltpu.make_async_copy(held.at[k], target, store_sem.at[k]))
+        stores[k].start()
+    for store in stores:
+        store.wait()
 
 
 def solution(mesh):
@@ -415,17 +454,25 @@
         rows += members
 
     def body(sol, res, direction, material, cond_table, cap_table, gas, supply):
-        vmem = pl.BlockSpec(memory_space=pltpu.VMEM)
-        smem = pl.BlockSpec(memory_space=pltpu.SMEM)
+        hbm = pl.BlockSpec(memory_space=pltpu.HBM)
         f32 = jnp.float32
-        block = jax.ShapeDtypeStruct(sol.shape, f32)
-        return pl.pallas_call(
+        block = jax.ShapeDtypeStruct((32, 8, 128), f32)
+        flat = [value.reshape(256, 128) for value in (res, direction)]
+        fields = pl.pallas_call(
             lambda *refs: kernel(sizes, stages, *refs),
             out_shape=(block, block, block),
-            in_specs=[smem, smem] + [vmem] * 6,
-            out_specs=(vmem, vmem, vmem),
+            in_specs=[hbm] * 8,
+            out_specs=(hbm, hbm, hbm),
             scratch_shapes=[
                 pltpu.VMEM((DIM, 256, 128), f32),
+                pltpu.VMEM((3, 32, 8, 128), f32),
+                pltpu.SemaphoreType.DMA((3,)),
+                pltpu.SMEM((8,), f32),
+                pltpu.SMEM((8,), f32),
+                pltpu.VMEM((256, 128), f32),
+                pltpu.VMEM((32, 8, 128), jnp.int32),
+                pltpu.VMEM((32, 128), f32),
+                pltpu.VMEM((32, 128), jnp.int32),
                 pltpu.VMEM((36, 8, 128), f32),
                 pltpu.VMEM((2, 32, 8, 128), f32),
                 pltpu.VMEM((2, 32, 8, 128), f32),
@@ -449,12 +496,26 @@
                 pltpu.SemaphoreType.DMA((sizes["gz"],)),
                 pltpu.SemaphoreType.DMA((rows,)),
                 pltpu.SemaphoreType.DMA((rows,)),
+                pltpu.SemaphoreType.DMA((8,)),
             ],
             compiler_params=pltpu.CompilerParams(
-                collective_id=0, has_side_effects=True, vmem_limit_bytes=32 * 1024 * 1024
+                collective_id=0, has_side_effects=True, vmem_limit_bytes=VMEM
             ),
             cost_estimate=pl.CostEstimate(flops=10**7, bytes_accessed=10**6, transcendentals=0),
-        )(cond_table, cap_table, sol, res, direction, material, gas, supply)
+        )(cond_table, cap_table, sol.reshape(32, 8, 128), *flat, material.reshape(32, 8, 128), gas, supply)
+        outs = pl.pallas_call(
+            finish,
+            out_shape=(block, block, block),
+            in_specs=[hbm] * 3,
+            out_specs=(hbm, hbm, hbm),
+            scratch_shapes=[
+                pltpu.VMEM((3, 32, 8, 128), f32),
+                pltpu.SemaphoreType.DMA((3,)),
+                pltpu.SemaphoreType.DMA((3,)),
+            ],
+            compiler_params=pltpu.CompilerParams(vmem_limit_bytes=VMEM),
+        )(fields[1], fields[2], fields[0])
+        return tuple(value.reshape(sol.shape) for value in (outs[2], outs[0], outs[1]))
 
     spec = P("gx", "gy", "gz")
     in_specs = (spec, spec, spec, spec, P(), P(), P("gy", "gz"), P("gy", "gz"))

time: 36.8 us -> 29 us (0.79)
  local copies, waits for them, and re-layouts: 8.32 us -> 0 us
  Pallas kernels: 27.5 us -> 28.2 us
    unnamed x19 -> x0, local copies, waits for them, and re-layouts: 8.32 us -> none
    pallas_call x0 -> x1, Pallas kernels: none -> 1.74 us  [body(): pl.pallas_call(finish, out_shape=(block, block, block), in_specs=[hbm] *...]
    pallas_call x1, Pallas kernels: 27.5 us -> 26.5 us  [body(): pl.pallas_call(lambda *refs: kernel(sizes, stages, *refs), out_shape=(blo...]
where the time goes in v2:
time: 29 us; the launch traced here: 28.8 us
  Pallas kernels  28.2 us (97%)
  between operations  0.64 us (2%)
    pallas_call x1, Pallas kernels, body(): pl.pallas_call(lambda *refs: kernel(sizes, stages, *refs), out_shape=(blo...  26.5 us
    pallas_call x1, Pallas kernels, body(): pl.pallas_call(finish, out_shape=(block, block, block), in_specs=[hbm] *...  1.74 us

profile of v2, /device:TPU:0, one launch (start us, length us, event | category | flops | bytes accessed | tf_op | source)
XLA Modules:
  0.0 28.8 jit_solution(10522921464427492545)
XLA Ops:
  0.6 26.5 %shard_map.103 = (f32[32,8,128]{2,1,0:T(8,128)}, f32[32,8,128]{2,1,0:T(8,128)}, f32[32,8,128]{2,1,0:T(8,128)}) custom-call(f32[8]{0:T(128)} %refs_0_.1, f32[8]{0:T(128)} %refs_1_.1, f32[32,8,128]{2,1,0:T(8,128)} %bitcast.7, f32[256,128]{1,0:T(8,128)} %bitcast.8, f32[256,128]{1,0:T(8,128)} %bitcast.9, s32[32,8,128]{2,1,0:T(8,128)} %bitcast.10, ...), custom_call_target="tpu_custom_call" | custom-call | flops 10000000 | bytes 1000000 | tf_op jit(solution)/shard_map/pallas_call | solution.py:461
  27.1 1.7 %shard_map.104 = (f32[32,8,128]{2,1,0:T(8,128)}, f32[32,8,128]{2,1,0:T(8,128)}, f32[32,8,128]{2,1,0:T(8,128)}) custom-call(f32[32,8,128]{2,1,0:T(8,128)} %get-tuple-element.9.res_in, f32[32,8,128]{2,1,0:T(8,128)} %get-tuple-element.10.dir_in, f32[32,8,128]{2,1,0:T(8,128)} %get-tuple-element.11.sol_in), custom_call_target="tpu_custom_call" | custom-call | tf_op jit(solution)/shard_map/pallas_call | solution.py:506
